TPU v7x, 32 devices: a whole 2x2x4 slice. The times are simulated.
32 devices in a mesh: groups: 2 (over y), blk: 4 (over z), heads: 2 (over x), section: 2 (over core).
Axes of the slice: x: 2, y: 2, z: 4, core: 2. Of those that a mesh axis runs over, the one named last changes fastest.
Arguments:
- dec_states: bfloat16 [4096, 2304], P(('groups', 'blk', 'section')), parts along dimension 0, may hold values from -6 to 6
- cross_keys: bfloat16 [1024, 1, 256], P(('groups', 'blk')), parts along dimension 0, may hold values from -15 to 15
- cross_values: bfloat16 [1024, 1, 256], P(('groups', 'blk')), parts along dimension 0, may hold values from -6 to 6
- attn_gain: float32 [2304], replicated, may hold values from 0.1 to 1.9
- query_weight: bfloat16 [2304, 512], P(None, 'heads'), may hold values from -0.125 to 0.125
- out_weight: bfloat16 [512, 2304], P('heads'), may hold values from -0.25 to 0.25
- post_attn_gain: float32 [2304], replicated, may hold values from 0.1 to 1.9
- ffn_gain: float32 [2304], replicated, may hold values from 0.1 to 1.9
- gate_weight: bfloat16 [2304, 9216], P('blk', ('heads', 'section')), may hold values from -0.125 to 0.125
- up_weight: bfloat16 [2304, 9216], P('blk', ('heads', 'section')), may hold values from -0.125 to 0.125
- down_weight: bfloat16 [9216, 2304], P(('heads', 'section'), 'blk'), may hold values from -0.0625 to 0.0625
- post_ffn_gain: float32 [2304], replicated, may hold values from 0.1 to 1.9
Outputs:
- scored_states: bfloat16 [4096, 2304], P(('groups', 'blk', 'heads', 'section')), parts along dimension 0
There are 2 independent parts, one for each index of `groups`. A program takes and returns all parts, laid end to end along the dimension named above; an argument that names none is the same for every part. Nothing has to cross between parts.
All inputs are finite; a program needn't handle non-finite values.
Results may differ from a plain program's by a relative error of at most 0.02.
Values may be sent and summed in bfloat16 or wider, within the bound.
No kernel may reach another device: no remote copies, remote signals or barrier semaphores. Data moves between devices by JAX's collectives and lax.ppermute only.
A program may use at most 128 MiB of HBM per device.

v0:
```python
import jax
import jax.numpy as jnp
from jax import lax
from jax.sharding import PartitionSpec as P

HD = 256
GROUP = 2
softcap_limit = 50.0


def from_partner(block, axis, bit):
    count = lax.axis_size(axis)
    route = []
    for low in range(count):
        high = low | 1 << bit
        if high != low and high < count:
            route += [(low, high), (high, low)]
    return lax.ppermute(block, axis, route)


def rms_scale(values, gain):
    return values * lax.rsqrt(jnp.mean(values * values, axis=-1, keepdims=True) + 1e-06) * gain


def capped_scores(queries, keys):
    raw = lax.dot_general(
        queries, keys, (((1,), (1,)), ((), ())), preferred_element_type=jnp.float32
    ) * HD ** (-0.5)
    return softcap_limit * jnp.tanh(raw / softcap_limit)


def body(
    dec_states,
    cross_keys,
    cross_values,
    attn_gain,
    query_weight,
    out_weight,
    post_attn_gain,
    ffn_gain,
    gate_weight,
    up_weight,
    down_weight,
    post_ffn_gain,
):
    head_index = lax.axis_index("heads")
    kv_index = head_index // GROUP
    keys_local = lax.dynamic_index_in_dim(cross_keys, kv_index, 1, keepdims=False)
    values_local = lax.dynamic_index_in_dim(cross_values, kv_index, 1, keepdims=False)
    gate_full, up_full, down_full = (
        lax.all_gather(gate_weight, "blk", axis=0, tiled=True),
        lax.all_gather(up_weight, "blk", axis=0, tiled=True),
        lax.all_gather(down_weight, "blk", axis=1, tiled=True),
    )
    states = dec_states.astype(jnp.float32)
    normed = rms_scale(states, attn_gain).astype(jnp.bfloat16)
    queries = jnp.dot(normed, query_weight, preferred_element_type=jnp.float32).astype(jnp.bfloat16)
    rows_here = queries.shape[0]
    probs = jnp.exp(capped_scores(queries, lax.all_gather(keys_local, "blk", axis=0, tiled=True)))
    numer = jnp.dot(
        probs.astype(jnp.bfloat16),
        lax.all_gather(values_local, "blk", axis=0, tiled=True),
        preferred_element_type=jnp.float32,
    )
    numer, denom = (numer, jnp.sum(probs, axis=1))
    context = (numer / denom[:, None]).astype(jnp.bfloat16)
    head_term = jnp.dot(context, out_weight, preferred_element_type=jnp.float32)
    attended = lax.psum(head_term.astype(jnp.bfloat16), "heads").astype(jnp.float32)
    residual = (states + rms_scale(attended, post_attn_gain)).astype(jnp.bfloat16)
    ffn_input = rms_scale(residual.astype(jnp.float32), ffn_gain).astype(jnp.bfloat16)
    section_size = lax.axis_size("section")
    section_index = lax.axis_index("section")
    out_rows = rows_here // lax.axis_size("heads")
    block_index = head_index * section_size + section_index
    ffn_rows = lax.all_gather(ffn_input, "section", axis=0, tiled=True)
    partner_block = head_index * section_size + (1 - section_index)
    send_start = jnp.clip(
        partner_block * out_rows - section_index * rows_here, 0, rows_here - out_rows
    )
    outgoing = lax.dynamic_slice_in_dim(residual, send_start, out_rows, 0)
    incoming = from_partner(outgoing, "section", 0)
    own_start = jnp.clip(
        block_index * out_rows - section_index * rows_here, 0, rows_here - out_rows
    )
    local_rows = lax.dynamic_slice_in_dim(residual, own_start, out_rows, 0)
    holder = block_index * out_rows // rows_here
    residual_out = jnp.where(holder == section_index, local_rows, incoming)
    gate = jnp.dot(ffn_rows, gate_full, preferred_element_type=jnp.float32)
    up_part = jnp.dot(ffn_rows, up_full, preferred_element_type=jnp.float32)
    hidden = (jax.nn.gelu(gate, approximate=True) * up_part).astype(jnp.bfloat16)
    terms = jnp.dot(hidden, down_full, preferred_element_type=jnp.float32)
    ffn_out = lax.psum_scatter(
        terms.astype(jnp.bfloat16), ("heads", "section"), scatter_dimension=0, tiled=True
    ).astype(jnp.float32)
    return (residual_out.astype(jnp.float32) + rms_scale(ffn_out, post_ffn_gain)).astype(
        jnp.bfloat16
    )


def solution(mesh):
    in_specs = (
        P(("groups", "blk", "section"), None),
        P(("groups", "blk"), None, None),
        P(("groups", "blk"), None, None),
        P(),
        P(None, "heads"),
        P("heads", None),
        P(),
        P(),
        P("blk", ("heads", "section")),
        P("blk", ("heads", "section")),
        P(("heads", "section"), "blk"),
        P(),
    )
    out_specs = P(("groups", "blk", "heads", "section"), None)
    return jax.shard_map(body, mesh=mesh, in_specs=in_specs, out_specs=out_specs, check_vma=False)
```

profile of v0, /device:TPU:0, one launch (start us, length us, event | category | flops | bytes accessed | tf_op | source)
XLA Modules:
  0.0 725.9 jit_solution(15588221195975664672)
XLA Ops:
  6.5 16.0 %all-gather = bf16[512,1,256]{2,0,1:T(8,128)(2,1)S(1)} all-gather(bf16[128,1,256]{2,0,1:T(8,128)(2,1)} %param.13), channel_id=2, replica_groups=mesh['groups'=2,'blk'=4,'heads'=2,'section'=2] {'blk'}, dimensions={0}, use_global_device_ids=true | all-gather | bytes 327680 | tf_op jit(solution)/shard_map/all_gather | solution.py:59
  22.5 1.6 fusion.13
  24.1 14.8 %all-gather.1 = bf16[512,1,256]{2,0,1:T(8,128)(2,1)S(1)} all-gather(bf16[128,1,256]{2,0,1:T(8,128)(2,1)} %param.14), channel_id=3, replica_groups=mesh['groups'=2,'blk'=4,'heads'=2,'section'=2] {'blk'}, dimensions={0}, use_global_device_ids=true | all-gather | bytes 327680 | tf_op jit(solution)/shard_map/all_gather | solution.py:62
  38.9 2.6 fusion.45
  41.4 0.0 copy-start.1
  41.5 1.7 convolution_convert_fusion.1
  43.2 0.0 all-reduce.2.cloned.1.call-update
  43.2 0.0 all-gather.7.cloned.1.call-start
  43.3 43.9 %all-reduce.2.cloned.1.call-done = bf16[256,2304]{1,0:T(8,128)(2,1)} async-done(((bf16[256,2304]{1,0:T(8,128)(2,1)}), bf16[256,2304]{1,0:T(8,128)(2,1)}) %all-reduce.2.cloned.1.call-update) | async-done | bytes 1179664 | tf_op jit(solution)/shard_map/psum | solution.py:68
  87.2 1.6 fusion.8
  88.8 2.0 fusion.10
  90.8 1.4 fusion.12
  92.2 0.0 all-gather.7.cloned.1.call-update
  92.2 0.0 all-gather.9.cloned.1.call-start
  92.3 0.7 all-gather.9.cloned.1.call-update
  93.0 0.0 all-gather.11.cloned.1.call-start
  93.0 0.5 all-gather.11.cloned.1.call-update
  93.5 0.0 all-gather.13.cloned.1.call-start
  93.6 0.5 all-gather.13.cloned.1.call-update
  94.1 0.0 reduce-scatter.2.cloned.1.call-start
  94.2 9.2 %all-gather.7.cloned.1.call-done = bf16[512,2304]{1,0:T(8,128)(2,1)} async-done(((bf16[256,2304]{1,0:T(8,128)(2,1)}), bf16[512,2304]{1,0:T(8,128)(2,1)}) %all-gather.7.cloned.1.call-update) | async-done | bytes 2359312 | tf_op jit(solution)/shard_map/all_gather | solution.py:75
  103.3 188.8 %all-gather.9.cloned.1.call-done = bf16[2304,2304]{1,0:T(8,128)(2,1)} async-done(((bf16[576,2304]{1,0:T(8,128)(2,1)}), bf16[2304,2304]{1,0:T(8,128)(2,1)}) %all-gather.9.cloned.1.call-update) | async-done | bytes 10616848 | tf_op jit(solution)/shard_map/all_gather | solution.py:51
  292.2 11.6 %fusion.48 = f32[512,2304]{1,0:T(8,128)} fusion(bf16[512,2304]{1,0:T(8,128)(2,1)} %all-gather.7.cloned.1.call-done, bf16[2304,2304]{1,0:T(8,128)(2,1)} %all-gather.9.cloned.1.call-done), kind=kOutput, calls=%fused_computation.58 | convolution fusion | flops 5435817984 | bytes 17694720 | tf_op jit(solution)/shard_map/dot_general | solution.py:88
  303.8 174.1 %all-gather.11.cloned.1.call-done = bf16[2304,2304]{1,0:T(8,128)(2,1)} async-done(((bf16[576,2304]{1,0:T(8,128)(2,1)}), bf16[2304,2304]{1,0:T(8,128)(2,1)}) %all-gather.11.cloned.1.call-update) | async-done | bytes 10616848 | tf_op jit(solution)/shard_map/all_gather | solution.py:52
  477.8 185.7 %all-gather.13.cloned.1.call-done = bf16[2304,2304]{0,1:T(8,128)(2,1)} async-done(((bf16[2304,576]{0,1:T(8,128)(2,1)}), bf16[2304,2304]{0,1:T(8,128)(2,1)}) %all-gather.13.cloned.1.call-update) | async-done | bytes 10616848 | tf_op jit(solution)/shard_map/all_gather | solution.py:53
  663.5 20.7 %convolution_convert_fusion = bf16[512,2304]{1,0:T(8,128)(2,1)} fusion(bf16[2304,2304]{0,1:T(8,128)(2,1)} %all-gather.13.cloned.1.call-done, bf16[512,2304]{1,0:T(8,128)(2,1)} %all-gather.7.cloned.1.call-done, bf16[2304,2304]{1,0:T(8,128)(2,1)} %all-gather.11.cloned.1.call-done, f32[512,2304]{1,0:T(8,128)} %fusion.48), kind=kOutput, calls=%fused_computation.10 | convolution fusion | flops 10884612096 | bytes 30670848 | tf_op jit(solution)/shard_map/dot_general | solution.py:91
  684.3 0.0 reduce-scatter.2.cloned.1.call-update
  684.3 0.1 constant_dynamic-slice_fusion
  684.5 0.1 collective-permute-start
  684.6 30.9 %reduce-scatter.2.cloned.1.call-done = bf16[128,2304]{1,0:T(8,128)(2,1)} async-done(((bf16[512,2304]{1,0:T(8,128)(2,1)}), bf16[128,2304]{1,0:T(8,128)(2,1)}) %reduce-scatter.2.cloned.1.call-update) | async-done | bytes 589840 | tf_op jit(solution)/shard_map/reduce_scatter | solution.py:92
  715.4 1.3 fusion.20
  716.7 2.3 fusion.23
  (13 shorter events, 0.1 us)
Async XLA Ops:
  6.5 34.9 %copy-start = (bf16[256,2304]{1,0:T(8,128)(2,1)S(1)}, bf16[256,2304]{1,0:T(8,128)(2,1)}, u32[]{:S(2)}) copy-start(bf16[256,2304]{1,0:T(8,128)(2,1)} %param.17) | copy-start | bytes 3538948
  6.5 80.7 %all-reduce.2.cloned.1.call-start = ((), (), s32[]{:S(2)}) async-start(), calls=%async_computation.1 | async-start | bytes 2359296 | tf_op jit(solution)/shard_map/psum | solution.py:68
  41.4 47.3 %copy-start.1 = (bf16[256,2304]{1,0:T(8,128)(2,1)S(1)}, bf16[256,2304]{1,0:T(8,128)(2,1)}, u32[]{:S(2)}) copy-start(bf16[256,2304]{1,0:T(8,128)(2,1)} %param.12) | copy-start | bytes 3538948
  43.2 47.6 %copy-start.2 = (f32[2304]{0:T(1024)S(1)}, f32[2304]{0:T(1024)}, u32[]{:S(2)}) copy-start(f32[2304]{0:T(1024)} %param.19) | copy-start | bytes 27652
  43.2 60.1 %all-gather.7.cloned.1.call-start = ((), (), s32[]{:S(2)}) async-start(), calls=%async_computation.2 | async-start | bytes 3538944 | tf_op jit(solution)/shard_map/all_gather | solution.py:75
  92.2 199.9 %all-gather.9.cloned.1.call-start = ((), (), s32[]{:S(2)}) async-start(), calls=%async_computation.3 | async-start | bytes 13271040 | tf_op jit(solution)/shard_map/all_gather | solution.py:51
  93.0 384.9 %all-gather.11.cloned.1.call-start = ((), (), s32[]{:S(2)}) async-start(), calls=%async_computation.4 | async-start | bytes 13271040 | tf_op jit(solution)/shard_map/all_gather | solution.py:52
  93.5 570.0 %all-gather.13.cloned.1.call-start = ((), (), s32[]{:S(2)}) async-start(), calls=%async_computation.5 | async-start | bytes 13271040 | tf_op jit(solution)/shard_map/all_gather | solution.py:53
  94.1 621.3 %reduce-scatter.2.cloned.1.call-start = ((), (), s32[]{:S(2)}) async-start(), calls=%async_computation.6 | async-start | bytes 2949120 | tf_op jit(solution)/shard_map/reduce_scatter | solution.py:92
  684.3 32.5 %copy-start.3 = (f32[2304]{0:T(1024)S(1)}, f32[2304]{0:T(1024)}, u32[]{:S(2)}) copy-start(f32[2304]{0:T(1024)} %param.23) | copy-start | bytes 27652
  684.5 32.3 %collective-permute-start = (bf16[128,2304]{1,0:T(8,128)(2,1)S(1)}, bf16[128,2304]{1,0:T(8,128)(2,1)S(1)}, u32[]{:S(2)}, u32[]{:S(2)}) collective-permute-start(bf16[128,2304]{1,0:T(8,128)(2,1)S(1)} %constant_dynamic-slice_fusion), channel_id=1, source_target_pairs={{0,1},{1,0},{2,3},{3,2},{4,5},{5,4},{6,7},{7,6},{8,9},{9,8},{10,11... | collective-permute-start | bytes 1769480 | tf_op jit(solution)/shard_map/ppermute | solution.py:18
Sparse Core Ops, SparseCore 0:
  43.3 43.8 all-reduce.1
  92.3 10.9 all-gather.6
  104.9 187.2 all-gather.8
  293.6 184.2 all-gather.10
  479.3 184.2 all-gather.12
  684.4 30.9 reduce-scatter.1
where the time goes:
time: 726 us
  waiting for transfers between devices  634 us (87%)
  matrix products  36.7 us (5%)
  blocking collectives  30.7 us (4%)
  between operations  13.6 us (2%)
  other arithmetic  10.1 us (1%)
    all_gather x1, waiting for transfers between devices, body(): lax.all_gather(gate_weight, 'blk', axis=0, tiled=True)  189 us
    all_gather x1, waiting for transfers between devices, body(): lax.all_gather(down_weight, 'blk', axis=1, tiled=True)  186 us
    all_gather x1, waiting for transfers between devices, body(): lax.all_gather(up_weight, 'blk', axis=0, tiled=True)  174 us
    psum x1, waiting for transfers between devices, body(): lax.psum(head_term.astype(jnp.bfloat16), 'heads').astype(jnp.float32)  43.9 us
    reduce_scatter x1, waiting for transfers between devices, body(): lax.psum_scatter(terms.astype(jnp.bfloat16), ('heads', 'section'), scatte...  30.9 us
    dot_general x1, matrix products, body(): terms = jnp.dot(hidden, down_full, preferred_element_type=jnp.float32)  20.7 us
    all_gather x1, blocking collectives, body(): lax.all_gather(keys_local, 'blk', axis=0, tiled=True)  16 us
    all_gather x1, blocking collectives, body(): lax.all_gather(values_local, 'blk', axis=0, tiled=True)  14.8 us
  transfers between devices with their start and end apart: 7, of which 6 were waited for; matrix products, arithmetic and copies ran while one was open for 2% of the time, Pallas kernels for 0%

commit v1 on v0

--- a/solution.py
+++ b/solution.py
@@ -6,6 +6,28 @@
 HD = 256
 GROUP = 2
 softcap_limit = 50.0
+
+
+def in_order(blocks, dim):
+    blocks = jnp.moveaxis(blocks, 0, dim)
+    dims = blocks.shape
+    return blocks.reshape(*dims[:dim], dims[dim] * dims[dim + 1], *dims[dim + 2 :])
+
+
+def collect(x, axis, dim):
+    peers = lax.axis_size(axis)
+    pairs = [(i, (i + 1) % peers) for i in range(peers)]
+    back = [(b, a) for a, b in pairs]
+    lower, upper = ([], [])
+    for step in range(peers - 1):
+        if step % 2 == 0:
+            lower.append(lax.ppermute(lower[-1] if lower else x, axis, pairs))
+        else:
+            upper.append(lax.ppermute(upper[-1] if upper else x, axis, back))
+    parts = jnp.stack([*lower[::-1], x, *upper])
+    shift = lax.axis_index(axis) - len(lower)
+    parts = parts[(jnp.arange(peers) - shift) % peers]
+    return in_order(parts, dim)
 
 
 def from_partner(block, axis, bit):
@@ -50,7 +72,7 @@
     gate_full, up_full, down_full = (
         lax.all_gather(gate_weight, "blk", axis=0, tiled=True),
         lax.all_gather(up_weight, "blk", axis=0, tiled=True),
-        lax.all_gather(down_weight, "blk", axis=1, tiled=True),
+        collect(down_weight, "blk", 1),
     )
     states = dec_states.astype(jnp.float32)
     normed = rms_scale(states, attn_gain).astype(jnp.bfloat16)

time: 726 us -> 687 us (0.946)
  waiting for transfers between devices: 634 us -> 467 us
  starting transfers between devices: 0.27 us -> 87.9 us
  local copies, waits for them, and re-layouts: 0.17 us -> 21.5 us
  other arithmetic: 10.1 us -> 29.1 us
    ppermute x0 -> x3, waiting for transfers between devices: none -> 237 us  [the longest x2 166 us: collect(): lower.append(lax.ppermute(lower[-1] if lower else x, axis, pairs))]
    all_gather x1, waiting for transfers between devices: 189 us -> 0.01 us  [body(): lax.all_gather(gate_weight, 'blk', axis=0, tiled=True)]
    all_gather x1 -> x0, waiting for transfers between devices: 186 us -> none  [body(): lax.all_gather(down_weight, 'blk', axis=1, tiled=True)]
    ppermute x0 -> x3, starting transfers between devices: none -> 87.7 us  [the longest x2 85.4 us: collect(): lower.append(lax.ppermute(lower[-1] if lower else x, axis, pairs))]
    gather x0 -> x3, local copies, waits for them, and re-layouts: none -> 21.3 us  [collect(): parts = parts[(jnp.arange(peers) - shift) % peers]]
    all_gather x1, waiting for transfers between devices: 174 us -> 155 us  [body(): lax.all_gather(up_weight, 'blk', axis=0, tiled=True)]
    unnamed x0 -> x1, other arithmetic: none -> 9.55 us
    another operation x0 -> x1, other arithmetic: none -> 9.43 us  [collect(): parts = jnp.stack([*lower[::-1], x, *upper])]
  transfers between devices with their start and end apart: 7 -> 9, of which waited for: 6 -> 6; matrix products, arithmetic and copies ran while one was open for 2% -> 8% of each run, Pallas kernels for 0% -> 0%
where the time goes in v1:
time: 687 us; the launch traced here: 686 us
  waiting for transfers between devices  467 us (68%)
  starting transfers between devices  87.9 us (13%)
  matrix products  36.7 us (5%)
  blocking collectives  30.7 us (4%)
  other arithmetic  29.1 us (4%)
  local copies, waits for them, and re-layouts  21.5 us (3%)
  between operations  13.3 us (2%)
    ppermute x2, waiting for transfers between devices, collect(): lower.append(lax.ppermute(lower[-1] if lower else x, axis, pairs))  166 us
    all_gather x1, waiting for transfers between devices, body(): lax.all_gather(up_weight, 'blk', axis=0, tiled=True)  155 us
    ppermute x2, starting transfers between devices, collect(): lower.append(lax.ppermute(lower[-1] if lower else x, axis, pairs))  85.4 us
    ppermute x1, waiting for transfers between devices, collect(): upper.append(lax.ppermute(upper[-1] if upper else x, axis, back))  70.2 us
    psum x1, waiting for transfers between devices, body(): lax.psum(head_term.astype(jnp.bfloat16), 'heads').astype(jnp.float32)  43.9 us
    reduce_scatter x1, waiting for transfers between devices, body(): lax.psum_scatter(terms.astype(jnp.bfloat16), ('heads', 'section'), scatte...  30.9 us
    gather x3, local copies, waits for them, and re-layouts, collect(): parts = parts[(jnp.arange(peers) - shift) % peers]  21.3 us
    dot_general x1, matrix products, body(): terms = jnp.dot(hidden, down_full, preferred_element_type=jnp.float32)  20.8 us
  transfers between devices with their start and end apart: 9, of which 6 were waited for; matrix products, arithmetic and copies ran while one was open for 8% of the time, Pallas kernels for 0%

profile of v1, /device:TPU:0, one launch (start us, length us, event | category | flops | bytes accessed | tf_op | source)
XLA Modules:
  0.0 686.4 jit_solution(5611901723703186765)
XLA Ops:
  6.5 16.0 %all-gather = bf16[512,1,256]{2,0,1:T(8,128)(2,1)S(1)} all-gather(bf16[128,1,256]{2,0,1:T(8,128)(2,1)} %param.13), channel_id=2, replica_groups=mesh['groups'=2,'blk'=4,'heads'=2,'section'=2] {'blk'}, dimensions={0}, use_global_device_ids=true | all-gather | bytes 327680 | tf_op jit(solution)/shard_map/all_gather | solution.py:81
  22.5 1.6 fusion.13
  24.1 14.8 %all-gather.1 = bf16[512,1,256]{2,0,1:T(8,128)(2,1)S(1)} all-gather(bf16[128,1,256]{2,0,1:T(8,128)(2,1)} %param.14), channel_id=3, replica_groups=mesh['groups'=2,'blk'=4,'heads'=2,'section'=2] {'blk'}, dimensions={0}, use_global_device_ids=true | all-gather | bytes 327680 | tf_op jit(solution)/shard_map/all_gather | solution.py:84
  38.9 2.6 fusion.48
  41.5 1.7 convolution_convert_fusion.1
  43.2 0.0 all-gather.6.cloned.1.call-start
  43.3 43.9 %all-reduce.2.cloned.1.call-done = bf16[256,2304]{1,0:T(8,128)(2,1)} async-done(((bf16[256,2304]{1,0:T(8,128)(2,1)}), bf16[256,2304]{1,0:T(8,128)(2,1)}) %all-reduce.2.cloned.1.call-update) | async-done | bytes 1179664 | tf_op jit(solution)/shard_map/psum | solution.py:90
  87.2 1.6 fusion.8
  88.8 2.0 fusion.10
  90.8 1.4 fusion.12
  92.2 0.0 all-gather.8.cloned.1.call-start
  92.3 0.7 all-gather.8.cloned.1.call-update
  93.0 0.5 all-gather.10.cloned.1.call-update
  93.6 1.5 collective-permute-start.1
  95.1 2.3 collective-permute-start.3
  97.4 94.2 %collective-permute-done.1 = bf16[2304,576]{0,1:T(8,128)(2,1)} collective-permute-done((bf16[2304,576]{0,1:T(8,128)(2,1)}, bf16[2304,576]{0,1:T(8,128)(2,1)}, u32[]{:S(2)}, u32[]{:S(2)}) %collective-permute-start.1) | collective-permute-done | bytes 2654240 | tf_op jit(solution)/shard_map/ppermute | solution.py:24
  191.6 83.8 %collective-permute-start.2 = (bf16[2304,576]{0,1:T(8,128)(2,1)}, bf16[2304,576]{0,1:T(8,128)(2,1)}, u32[]{:S(2)}, u32[]{:S(2)}) collective-permute-start(bf16[2304,576]{0,1:T(8,128)(2,1)} %collective-permute-done.1), channel_id=1, source_target_pairs={{0,4},{4,8},{8,12},{12,0},{1,5},{5,9},{9,13},{13,1},{2,6},{6,10},{... | collective-permute-start | bytes 7962632 | tf_op jit(solution)/shard_map/ppermute | solution.py:24
  275.4 70.2 %collective-permute-done.3 = bf16[2304,576]{0,1:T(8,128)(2,1)} collective-permute-done((bf16[2304,576]{0,1:T(8,128)(2,1)}, bf16[2304,576]{0,1:T(8,128)(2,1)}, u32[]{:S(2)}, u32[]{:S(2)}) %collective-permute-start.3) | collective-permute-done | bytes 2654240 | tf_op jit(solution)/shard_map/ppermute | solution.py:26
  345.6 72.2 %collective-permute-done.2 = bf16[2304,576]{0,1:T(8,128)(2,1)} collective-permute-done((bf16[2304,576]{0,1:T(8,128)(2,1)}, bf16[2304,576]{0,1:T(8,128)(2,1)}, u32[]{:S(2)}, u32[]{:S(2)}) %collective-permute-start.2) | collective-permute-done | bytes 2654240 | tf_op jit(solution)/shard_map/ppermute | solution.py:24
  417.8 9.4 %pad_maximum_fusion = bf16[4,2304,576]{1,2,0:T(8,128)(2,1)} fusion(bf16[1,2304,576]{1,2,0:T(8,128)(2,1)} %bitcast.5, bf16[1,2304,576]{1,2,0:T(8,128)(2,1)} %bitcast.27, bf16[1,2304,576]{1,2,0:T(8,128)(2,1)} %bitcast.3, bf16[1,2304,576]{1,2,0:T(8,128)(2,1)} %bitcast.2), kind=kLoop, calls=%fused_computation.2 | loop fusion | flops 15925248 | bytes 21233664 | tf_op jit(solution)/shard_map/stack | solution.py:27
  427.3 8.9 %fusion.47 = (bf16[4,1152,576]{1,2,0:T(8,128)(2,1)}, bf16[4,1152,576]{1,2,0:T(8,128)(2,1)}) fusion(bf16[4,2304,576]{1,2,0:T(8,128)(2,1)} %pad_maximum_fusion), kind=kLoop, calls=%fused_computation.68 | loop fusion | bytes 21233664 | tf_op jit(solution)/shard_map/gather | solution.py:29
  436.2 6.0 gather_fusion
  442.2 6.4 gather_fusion.1
  448.6 9.6 %pad_maximum_fusion.1 = bf16[4,2304,576]{1,2,0:T(8,128)(2,1)} fusion(bf16[4,1152,576]{1,2,0:T(8,128)(2,1)} %gather_fusion.1, bf16[4,1152,576]{1,2,0:T(8,128)(2,1)} %gather_fusion), kind=kLoop, calls=%fused_computation.3 | loop fusion | flops 21233664 | bytes 21233664
  458.1 11.7 %fusion.51 = f32[512,2304]{1,0:T(8,128)} fusion(bf16[512,2304]{1,0:T(8,128)(2,1)} %all-gather.6.cloned.1.call-done, bf16[2304,2304]{1,0:T(8,128)(2,1)} %all-gather.8.cloned.1.call-done), kind=kOutput, calls=%fused_computation.70 | convolution fusion | flops 5435817984 | bytes 17694720 | tf_op jit(solution)/shard_map/dot_general | solution.py:110
  469.8 154.5 %all-gather.10.cloned.1.call-done = bf16[2304,2304]{1,0:T(8,128)(2,1)} async-done(((bf16[576,2304]{1,0:T(8,128)(2,1)}), bf16[2304,2304]{1,0:T(8,128)(2,1)}) %all-gather.10.cloned.1.call-update) | async-done | bytes 10616848 | tf_op jit(solution)/shard_map/all_gather | solution.py:74
  624.3 20.8 %convolution_convert_fusion = bf16[512,2304]{1,0:T(8,128)(2,1)} fusion(bf16[2304,2304]{0,1:T(8,128)(2,1)} %bitcast.26, bf16[512,2304]{1,0:T(8,128)(2,1)} %all-gather.6.cloned.1.call-done, bf16[2304,2304]{1,0:T(8,128)(2,1)} %all-gather.10.cloned.1.call-done, f32[512,2304]{1,0:T(8,128)} %fusion.51), kind=kOutput, calls=%fused_computation.14 | convolution fusion | flops 10884612096 | bytes 30670848 | tf_op jit(solution)/shard_map/dot_general | solution.py:113
  645.1 0.1 constant_dynamic-slice_fusion
  645.3 0.1 collective-permute-start
  645.4 30.9 %reduce-scatter.2.cloned.1.call-done = bf16[128,2304]{1,0:T(8,128)(2,1)} async-done(((bf16[512,2304]{1,0:T(8,128)(2,1)}), bf16[128,2304]{1,0:T(8,128)(2,1)}) %reduce-scatter.2.cloned.1.call-update) | async-done | bytes 589840 | tf_op jit(solution)/shard_map/reduce_scatter | solution.py:114
  676.3 1.3 fusion.20
  677.5 2.3 fusion.23
  (27 shorter events, 0.2 us)
Async XLA Ops:
  6.5 34.9 %copy-start = (bf16[256,2304]{1,0:T(8,128)(2,1)S(1)}, bf16[256,2304]{1,0:T(8,128)(2,1)}, u32[]{:S(2)}) copy-start(bf16[256,2304]{1,0:T(8,128)(2,1)} %param.17) | copy-start | bytes 3538948
  6.5 80.7 %all-reduce.2.cloned.1.call-start = ((), (), s32[]{:S(2)}) async-start(), calls=%async_computation.1 | async-start | bytes 2359296 | tf_op jit(solution)/shard_map/psum | solution.py:90
  41.4 47.4 %copy-start.2 = (bf16[256,2304]{1,0:T(8,128)(2,1)S(1)}, bf16[256,2304]{1,0:T(8,128)(2,1)}, u32[]{:S(2)}) copy-start(bf16[256,2304]{1,0:T(8,128)(2,1)} %param.12) | copy-start | bytes 3538948
  41.4 47.4 %copy-start.5 = (f32[2304]{0:T(1024)S(1)}, f32[2304]{0:T(1024)}, u32[]{:S(2)}) copy-start(f32[2304]{0:T(1024)} %param.18) | copy-start | bytes 27652
  43.2 47.6 %copy-start.3 = (f32[2304]{0:T(1024)S(1)}, f32[2304]{0:T(1024)}, u32[]{:S(2)}) copy-start(f32[2304]{0:T(1024)} %param.19) | copy-start | bytes 27652
  43.2 414.9 %all-gather.6.cloned.1.call-start = ((), (), s32[]{:S(2)}) async-start(), calls=%async_computation.2 | async-start | bytes 3538944 | tf_op jit(solution)/shard_map/all_gather | solution.py:97
  92.2 365.9 %all-gather.8.cloned.1.call-start = ((), (), s32[]{:S(2)}) async-start(), calls=%async_computation.3 | async-start | bytes 13271040 | tf_op jit(solution)/shard_map/all_gather | solution.py:73
  92.9 531.4 %all-gather.10.cloned.1.call-start = ((), (), s32[]{:S(2)}) async-start(), calls=%async_computation.4 | async-start | bytes 13271040 | tf_op jit(solution)/shard_map/all_gather | solution.py:74
  93.5 582.7 %reduce-scatter.2.cloned.1.call-start = ((), (), s32[]{:S(2)}) async-start(), calls=%async_computation.5 | async-start | bytes 2949120 | tf_op jit(solution)/shard_map/reduce_scatter | solution.py:114
  93.6 98.0 %collective-permute-start.1 = (bf16[2304,576]{0,1:T(8,128)(2,1)}, bf16[2304,576]{0,1:T(8,128)(2,1)}, u32[]{:S(2)}, u32[]{:S(2)}) collective-permute-start(bf16[2304,576]{0,1:T(8,128)(2,1)} %param.22), channel_id=1, source_target_pairs={{0,4},{4,8},{8,12},{12,0},{1,5},{5,9},{9,13},{13,1},{2,6},{6,10},{... | collective-permute-start | bytes 7962632 | tf_op jit(solution)/shard_map/ppermute | solution.py:24
  95.1 250.5 %collective-permute-start.3 = (bf16[2304,576]{0,1:T(8,128)(2,1)}, bf16[2304,576]{0,1:T(8,128)(2,1)}, u32[]{:S(2)}, u32[]{:S(2)}) collective-permute-start(bf16[2304,576]{0,1:T(8,128)(2,1)} %param.22), channel_id=1, source_target_pairs={{4,0},{8,4},{12,8},{0,12},{5,1},{9,5},{13,9},{1,13},{6,2},{10,6},{... | collective-permute-start | bytes 7962632 | tf_op jit(solution)/shard_map/ppermute | solution.py:26
  191.6 226.2 %collective-permute-start.2 = (bf16[2304,576]{0,1:T(8,128)(2,1)}, bf16[2304,576]{0,1:T(8,128)(2,1)}, u32[]{:S(2)}, u32[]{:S(2)}) collective-permute-start(bf16[2304,576]{0,1:T(8,128)(2,1)} %collective-permute-done.1), channel_id=1, source_target_pairs={{0,4},{4,8},{8,12},{12,0},{1,5},{5,9},{9,13},{13,1},{2,6},{6,10},{... | collective-permute-start | bytes 7962632 | tf_op jit(solution)/shard_map/ppermute | solution.py:24
  645.1 32.5 %copy-start.4 = (f32[2304]{0:T(1024)S(1)}, f32[2304]{0:T(1024)}, u32[]{:S(2)}) copy-start(f32[2304]{0:T(1024)} %param.23) | copy-start | bytes 27652
  645.1 34.7 %copy-start.1 = (bf16[256,2304]{1,0:T(8,128)(2,1)S(1)}, bf16[256,2304]{1,0:T(8,128)(2,1)}, u32[]{:S(2)}) copy-start(bf16[256,2304]{1,0:T(8,128)(2,1)} %param.17) | copy-start | bytes 3538948
  645.3 32.2 %collective-permute-start = (bf16[128,2304]{1,0:T(8,128)(2,1)S(1)}, bf16[128,2304]{1,0:T(8,128)(2,1)S(1)}, u32[]{:S(2)}, u32[]{:S(2)}) collective-permute-start(bf16[128,2304]{1,0:T(8,128)(2,1)S(1)} %constant_dynamic-slice_fusion), channel_id=1, source_target_pairs={{0,1},{1,0},{2,3},{3,2},{4,5},{5,4},{6,7},{7,6},{8,9},{9,8},{10,11... | collective-permute-start | bytes 1769480 | tf_op jit(solution)/shard_map/ppermute | solution.py:40
Sparse Core Ops, SparseCore 0:
  43.3 43.8 all-reduce.1
  92.3 10.9 all-gather.5
  104.9 334.5 all-gather.7
  440.9 183.3 all-gather.9
  645.2 30.9 reduce-scatter.1
